TPU v7x, 32 devices: a whole 2x2x4 slice. The times are simulated.
32 devices in a mesh: groups: 2 (over y), freq: 16 (over z, x, core).
Axes of the slice: x: 2, y: 2, z: 4, core: 2. Of those that a mesh axis runs over, the one named last changes fastest.
Arguments:
- refl: bfloat16 [128, 2, 512, 512], P(('groups', 'freq')), parts along dimension 0, may hold values from -0.1875 to 0.1875
- refl_scale: float32 [128, 4], P(('groups', 'freq')), parts along dimension 0, may hold values from 0.5 to 4
- freq_index: int32 [128], P(('groups', 'freq')), parts along dimension 0, may hold values from 1 to 1023, as said below
- fd_plus: bfloat16 [4096, 32, 512], P(('groups', 'freq')), parts along dimension 0, may hold values from -6 to 6
- onset: int32 [32768], P(('groups', 'freq')), parts along dimension 0, may hold values from 128 to 767
Outputs:
- f_minus: bfloat16 [4096, 32, 512], P(('groups', 'freq')), parts along dimension 0
- f_plus: float32 [4096, 32, 512], P(('groups', 'freq')), parts along dimension 0
There are 2 independent parts, one for each index of `groups`. A program takes and returns all parts, laid end to end along the dimension named above; each array names one. Nothing has to cross between parts.
Inputs may be any that keep to these rules, and one draw needn't show every extreme that they name: `freq_index`: the bins are distinct and ascending; the first is 1 and the last is 1023.
All inputs are finite; a program needn't handle non-finite values.
Results may differ from a plain program's by a relative error of at most 0.01.
Values may be sent and summed in bfloat16 or wider, within the bound.
No kernel may reach another device: no remote copies, remote signals or barrier semaphores. Data moves between devices by JAX's collectives and lax.ppermute only.
A program may use at most 128 MiB of HBM per device.

v0:
```python
import math
import jax
import jax.numpy as jnp
from jax import lax
from jax.sharding import PartitionSpec as P


def to_columns(field):
    return lax.all_to_all(field, "freq", split_axis=1, concat_axis=0, tiled=True)


def to_time(field):
    return lax.all_to_all(field, "freq", split_axis=0, concat_axis=1, tiled=True)


def local(refl, refl_scale, freq_index, fd_plus, onset):
    nfreq_dev = refl.shape[0]
    nrec = refl.shape[2]
    t_dev, points, _ = fd_plus.shape
    columns = points * nrec
    nshard = lax.axis_size("freq")
    ntime = t_dev * nshard
    width = columns // nshard
    first_col = lax.axis_index("freq") * width
    bins, scales = (
        lax.all_gather(freq_index, "freq", axis=0, tiled=True),
        lax.all_gather(refl_scale, "freq", axis=0, tiled=True),
    )
    nblocks = scales.shape[1]
    times = jnp.arange(ntime, dtype=jnp.int32)
    phase = bins[:, None] * times[None, :] % ntime
    angle = phase.astype(jnp.float32) * jnp.float32(2.0 * math.pi / ntime)
    cosine = jnp.cos(angle).astype(jnp.bfloat16)
    sine = jnp.sin(angle).astype(jnp.bfloat16)
    col_ids = first_col + jnp.arange(width, dtype=jnp.int32)
    block_ids = col_ids % nrec // (nrec // nblocks)
    onehot = (block_ids[None, :] == jnp.arange(nblocks, dtype=jnp.int32)[:, None]).astype(
        jnp.float32
    )
    col_scale = jnp.dot(
        scales, onehot, precision=lax.Precision.HIGHEST, preferred_element_type=jnp.float32
    )
    signed = jnp.where(times < ntime // 2, times, times - ntime)
    keep = (jnp.abs(signed)[:, None] < onset[None, :]).astype(jnp.float32)
    contract_time = (((0,), (0,)), ((), ()))

    def forward(colfield, table_c, table_s):
        real = jnp.dot(table_c, colfield, preferred_element_type=jnp.float32)
        imag = -jnp.dot(table_s, colfield, preferred_element_type=jnp.float32)
        spectrum = jnp.stack(
            [(real * col_scale).astype(jnp.bfloat16), (imag * col_scale).astype(jnp.bfloat16)],
            axis=1,
        )
        return lax.all_to_all(spectrum, "freq", split_axis=0, concat_axis=2, tiled=True)

    def convolve(spectrum, sign):
        spectrum = spectrum.reshape(nfreq_dev, 2, points, nrec)
        spec_r = spectrum[:, 0]
        spec_i = spectrum[:, 1]
        resp_r = refl[:, 0]
        resp_i = refl[:, 1]

        def apply(resp, spec):
            return jnp.einsum("frs,fvs->fvr", resp, spec, preferred_element_type=jnp.float32)

        out_r = apply(resp_r, spec_r) - sign * apply(resp_i, spec_i)
        out_i = apply(resp_r, spec_i) + sign * apply(resp_i, spec_r)
        stacked = jnp.stack([out_r.astype(jnp.bfloat16), out_i.astype(jnp.bfloat16)], axis=1)
        return lax.all_to_all(
            stacked.reshape(nfreq_dev, 2, columns), "freq", split_axis=2, concat_axis=0, tiled=True
        )

    def inverse(spectrum):
        trace = lax.dot_general(
            cosine, spectrum[:, 0], contract_time, preferred_element_type=jnp.float32
        )
        trace = trace - lax.dot_general(
            sine, spectrum[:, 1], contract_time, preferred_element_type=jnp.float32
        )
        return (trace * jnp.float32(2.0 / ntime) * keep).astype(jnp.bfloat16)

    direct = fd_plus.reshape(t_dev, columns)
    minus_cols = inverse(convolve(forward(to_columns(direct), cosine, sine), 1.0))
    minus_time = to_time(minus_cols)
    update_cols = inverse(convolve(forward(minus_cols, cosine, sine), -1.0))
    plus_time = direct.astype(jnp.float32) + to_time(update_cols).astype(jnp.float32)
    return (minus_time.reshape(t_dev, points, nrec), plus_time.reshape(t_dev, points, nrec))


def solution(mesh):
    return jax.shard_map(
        local,
        mesh=mesh,
        in_specs=(
            P(("groups", "freq"), None, None, None),
            P(("groups", "freq"), None),
            P(("groups", "freq")),
            P(("groups", "freq"), None, None),
            P(("groups", "freq")),
        ),
        out_specs=(P(("groups", "freq"), None, None), P(("groups", "freq"), None, None)),
        check_vma=False,
    )
```

profile of v0, /device:TPU:11, one launch (start us, length us, event | category | flops | bytes accessed | tf_op | source)
XLA Modules:
  0.0 541.2 jit_solution(8030469073627968279)
XLA Ops:
  0.6 7.9 %copy.51 = bf16[128,32,512]{0,2,1:T(8,128)(2,1)} copy(bf16[128,32,512]{2,1,0:T(8,128)(2,1)} %param.8) | data formatting | bytes 8388608 | tf_op args[3]
  8.5 6.7 %all-to-all-start = ((bf16[128,16,1024]{0,2,1:T(8,128)(2,1)}), bf16[128,16,1024]{0,2,1:T(8,128)(2,1)}, u32[]{:S(2)}, u32[]{:S(2)}) async-start(bf16[128,16,1024]{0,2,1:T(8,128)(2,1)} %bitcast.126), calls=%async_computation | async-start | bytes 8388608 | tf_op jit(solution)/shard_map/all_to_all | solution.py:9
  16.7 88.9 %all-reduce = s32[64]{0:T(128)S(1)} all-reduce(s32[64]{0:T(128)S(1)} %dynamic-update-slice), channel_id=1, replica_groups=mesh['groups'=2,'freq'=16] {'freq'}, use_global_device_ids=true, to_apply=%add | all-reduce | flops 64 | bytes 512
  105.6 18.6 %all-gather = f32[16,4,4]{2,1,0:T(4,128)S(1)} all-gather(f32[1,4,4]{2,1,0:T(4,128)S(1)} %bitcast.140), channel_id=1, replica_groups=mesh['groups'=2,'freq'=16] {'freq'}, dimensions={0}, use_global_device_ids=true | all-gather | bytes 1088 | tf_op jit(solution)/shard_map/all_gather | solution.py:27
  124.5 6.4 %copy.52 = bf16[16,128,1024]{2,1,0:T(8,128)(2,1)} copy(bf16[16,128,1024]{1,2,0:T(8,128)(2,1)} %bitcast.2) | data formatting | bytes 8388608 | tf_op jit(solution)/shard_map/all_to_all | solution.py:9
  130.9 4.5 fusion.64
  138.2 15.2 %all_to_all.114 = bf16[64,2,1024]{2,1,0:T(2,128)(2,1)S(1)} all-to-all(bf16[64,2,1024]{2,1,0:T(2,128)(2,1)S(1)} %copy.53), channel_id=1, replica_groups=mesh['groups'=2,'freq'=16] {'freq'}, dimensions={0} | all-to-all | bytes 524288 | tf_op jit(solution)/shard_map/all_to_all | solution.py:54
  161.9 13.0 %copy.57 = bf16[4,2,16384]{0,1,2:T(2,128)(2,1)} copy(bf16[4,2,16384]{2,0,1:T(4,128)(2,1)S(1)} %pad_maximum_fusion.1) | data formatting | bytes 524288 | tf_op jit(solution)/shard_map/stack | solution.py:68
  174.9 16.8 %reshape.93 = bf16[16,2,4096]{2,1,0:T(2,128)(2,1)} reshape(bf16[16384,2,4]{2,1,0:T(2,128)(2,1)} %bitcast.122) | data formatting | bytes 524288
  191.7 6.1 %all-to-all-start.2 = ((bf16[16,2,4096]{2,1,0:T(2,128)(2,1)}), bf16[16,2,4096]{2,1,0:T(2,128)(2,1)S(1)}, u32[]{:S(2)}, u32[]{:S(2)}) async-start(bf16[16,2,4096]{2,1,0:T(2,128)(2,1)} %reshape.93), calls=%async_computation.2 | async-start | bytes 524288 | tf_op jit(solution)/shard_map/all_to_all | solution.py:69
  197.8 7.9 %all-to-all-done.2 = bf16[16,2,4096]{2,1,0:T(2,128)(2,1)S(1)} async-done(((bf16[16,2,4096]{2,1,0:T(2,128)(2,1)}), bf16[16,2,4096]{2,1,0:T(2,128)(2,1)S(1)}, u32[]{:S(2)}, u32[]{:S(2)}) %all-to-all-start.2) | async-done | bytes 262176 | tf_op jit(solution)/shard_map/all_to_all | solution.py:69
  205.7 19.0 %reshape.94 = bf16[16384,2,4]{2,1,0:T(2,128)(2,1)} reshape(bf16[16,2,4096]{2,1,0:T(2,128)(2,1)S(1)} %all-to-all-done.2) | data formatting | bytes 524288
  224.7 11.9 %copy.67 = bf16[4,2,16,1024]{3,2,1,0:T(8,128)(2,1)S(1)} copy(bf16[4,2,16,1024]{0,1,3,2:T(2,128)(2,1)} %bitcast.123) | data formatting | bytes 524288 | tf_op jit(solution)/shard_map/all_to_all | solution.py:69
  240.4 4.1 fusion
  249.9 13.0 %all_to_all.115 = bf16[64,2,1024]{2,1,0:T(2,128)(2,1)S(1)} all-to-all(bf16[64,2,1024]{2,1,0:T(2,128)(2,1)S(1)} %copy.61), channel_id=1, replica_groups=mesh['groups'=2,'freq'=16] {'freq'}, dimensions={0} | all-to-all | bytes 524288 | tf_op jit(solution)/shard_map/all_to_all | solution.py:54
  271.4 13.0 %copy.63 = bf16[4,2,16384]{0,1,2:T(2,128)(2,1)} copy(bf16[4,2,16384]{2,0,1:T(4,128)(2,1)S(1)} %pad_maximum_fusion.3) | data formatting | bytes 524288 | tf_op jit(solution)/shard_map/stack | solution.py:68
  284.4 16.2 %reshape.95 = bf16[16,2,4096]{2,1,0:T(2,128)(2,1)S(1)} reshape(bf16[16384,2,4]{2,1,0:T(2,128)(2,1)} %bitcast.124) | data formatting | bytes 524288
  300.6 12.8 %all_to_all.116 = bf16[16,2,4096]{2,1,0:T(2,128)(2,1)S(1)} all-to-all(bf16[16,2,4096]{2,1,0:T(2,128)(2,1)S(1)} %reshape.95), channel_id=1, replica_groups=mesh['groups'=2,'freq'=16] {'freq'}, dimensions={0} | all-to-all | bytes 524288 | tf_op jit(solution)/shard_map/all_to_all | solution.py:69
  313.4 6.5 %all-to-all-start.3 = ((bf16[16,128,1024]{2,1,0:T(8,128)(2,1)}), bf16[16,128,1024]{2,1,0:T(8,128)(2,1)}, u32[]{:S(2)}, u32[]{:S(2)}) async-start(bf16[16,128,1024]{2,1,0:T(8,128)(2,1)} %bitcast.127), calls=%async_computation.3 | async-start | bytes 8388608 | tf_op jit(solution)/shard_map/all_to_all | solution.py:13
  319.9 19.1 %reshape.96 = bf16[16384,2,4]{2,1,0:T(2,128)(2,1)} reshape(bf16[16,2,4096]{2,1,0:T(2,128)(2,1)S(1)} %all_to_all.116) | data formatting | bytes 524288
  338.9 11.9 %copy.68 = bf16[4,2,16,1024]{3,2,1,0:T(8,128)(2,1)S(1)} copy(bf16[4,2,16,1024]{0,1,3,2:T(2,128)(2,1)} %bitcast.125) | data formatting | bytes 524288 | tf_op jit(solution)/shard_map/all_to_all | solution.py:69
  351.5 3.1 fusion.72
  354.6 4.9 fusion.1
  359.5 52.8 %all-to-all-done.3 = bf16[16,128,1024]{2,1,0:T(8,128)(2,1)} async-done(((bf16[16,128,1024]{2,1,0:T(8,128)(2,1)}), bf16[16,128,1024]{2,1,0:T(8,128)(2,1)}, u32[]{:S(2)}, u32[]{:S(2)}) %all-to-all-start.3) | async-done | bytes 4194336 | tf_op jit(solution)/shard_map/all_to_all | solution.py:13
  412.4 5.2 all-to-all-start.6
  417.6 6.5 %copy.60 = bf16[128,16,1024]{2,1,0:T(8,128)(2,1)} copy(bf16[128,16,1024]{2,0,1:T(8,128)(2,1)} %bitcast.19) | data formatting | bytes 8388608 | tf_op jit(solution)/shard_map/all_to_all | solution.py:13
  424.1 7.1 %reshape.83 = bf16[128,32,512]{2,1,0:T(8,128)(2,1)} reshape(bf16[128,16,1024]{2,1,0:T(8,128)(2,1)} %copy.60) | data formatting | bytes 8388608 | tf_op jit(solution)/shard_map/reshape | solution.py:87
  431.2 78.7 %all-to-all-done.6 = bf16[16,128,1024]{2,1,0:T(8,128)(2,1)} async-done(((bf16[16,128,1024]{2,1,0:T(8,128)(2,1)}), bf16[16,128,1024]{2,1,0:T(8,128)(2,1)}, u32[]{:S(2)}, u32[]{:S(2)}) %all-to-all-start.6) | async-done | bytes 4194336 | tf_op jit(solution)/shard_map/all_to_all | solution.py:13
  509.9 3.2 convert_bitcast_fusion
  513.2 8.3 %copy.66 = f32[128,16,1024]{2,1,0:T(8,128)} copy(f32[128,16,1024]{2,0,1:T(8,128)S(1)} %convert_bitcast_fusion) | data formatting | bytes 16777216 | tf_op jit(solution)/shard_map/convert_element_type | solution.py:86
  521.4 9.3 %reshape.85 = f32[128,32,512]{2,1,0:T(8,128)} reshape(f32[128,16,1024]{2,1,0:T(8,128)} %copy.66) | data formatting | bytes 16777216 | tf_op jit(solution)/shard_map/convert_element_type | solution.py:86
  530.7 10.2 %convert_add_fusion = f32[128,32,512]{2,1,0:T(8,128)} fusion(f32[128,32,512]{2,1,0:T(8,128)} %reshape.85, bf16[128,32,512]{2,1,0:T(8,128)(2,1)} %param.8), kind=kLoop, calls=%fused_computation.5 | loop fusion | flops 4194304 | bytes 20971520 | tf_op jit(solution)/shard_map/add | solution.py:86
  (53 shorter events, 30.4 us)
Async XLA Ops:
  8.5 6.7 %copy-start.7 = (u32[32]{0:T(128)S(1)}, u32[32]{0:T(128)}, u32[]{:S(2)}) copy-start(u32[32]{0:T(128)} %constant.68) | copy-start | bytes 388
  8.5 8.0 %copy-start.6 = (s32[4]{0:T(128)S(1)}, s32[4]{0:T(128)}, u32[]{:S(2)}) copy-start(s32[4]{0:T(128)} %param.7) | copy-start | bytes 52
  8.5 97.1 %copy-start.4 = (f32[4,4]{1,0:T(4,128)S(1)}, f32[4,4]{1,0:T(4,128)}, u32[]{:S(2)}) copy-start(f32[4,4]{1,0:T(4,128)} %param.6) | copy-start | bytes 196
  8.5 115.9 %all-to-all-start = ((bf16[128,16,1024]{0,2,1:T(8,128)(2,1)}), bf16[128,16,1024]{0,2,1:T(8,128)(2,1)}, u32[]{:S(2)}, u32[]{:S(2)}) async-start(bf16[128,16,1024]{0,2,1:T(8,128)(2,1)} %bitcast.126), calls=%async_computation | async-start | bytes 8388608 | tf_op jit(solution)/shard_map/all_to_all | solution.py:9
  130.9 4.5 copy-start.3
  153.7 4.8 copy-start
  191.7 14.0 %all-to-all-start.2 = ((bf16[16,2,4096]{2,1,0:T(2,128)(2,1)}), bf16[16,2,4096]{2,1,0:T(2,128)(2,1)S(1)}, u32[]{:S(2)}, u32[]{:S(2)}) async-start(bf16[16,2,4096]{2,1,0:T(2,128)(2,1)} %reshape.93), calls=%async_computation.2 | async-start | bytes 524288 | tf_op jit(solution)/shard_map/all_to_all | solution.py:69
  237.3 3.1 copy-start.5
  244.5 5.1 copy-start.2
  263.2 4.8 copy-start.1
  313.4 99.0 %all-to-all-start.3 = ((bf16[16,128,1024]{2,1,0:T(8,128)(2,1)}), bf16[16,128,1024]{2,1,0:T(8,128)(2,1)}, u32[]{:S(2)}, u32[]{:S(2)}) async-start(bf16[16,128,1024]{2,1,0:T(8,128)(2,1)} %bitcast.127), calls=%async_computation.3 | async-start | bytes 8388608 | tf_op jit(solution)/shard_map/all_to_all | solution.py:13
  412.4 97.6 %all-to-all-start.6 = ((bf16[16,128,1024]{2,1,0:T(8,128)(2,1)}), bf16[16,128,1024]{2,1,0:T(8,128)(2,1)}, u32[]{:S(2)}, u32[]{:S(2)}) async-start(bf16[16,128,1024]{2,1,0:T(8,128)(2,1)} %bitcast.128), calls=%async_computation.6 | async-start | bytes 8388608 | tf_op jit(solution)/shard_map/all_to_all | solution.py:13
where the time goes:
time: 550 us; the launch traced here: 541 us
  local copies, waits for them, and re-layouts  170 us (31%)
  blocking collectives  149 us (27%)
  waiting for transfers between devices  139 us (25%)
  matrix products  43.1 us (8%)
  starting transfers between devices  24.6 us (4%)
  other arithmetic  13.8 us (3%)
    all_to_all x2, waiting for transfers between devices, to_time(): lax.all_to_all(field, 'freq', split_axis=0, concat_axis=1, tiled=True)  132 us
    unnamed x1, blocking collectives  88.9 us
    unnamed x24, local copies, waits for them, and re-layouts  79.9 us
    all_to_all x2, blocking collectives, forward(): lax.all_to_all(spectrum, 'freq', split_axis=0, concat_axis=2, tiled=True)  28.2 us
    another operation x6, local copies, waits for them, and re-layouts, convolve(): jnp.stack([out_r.astype(jnp.bfloat16), out_i.astype(jnp.bfloat16)], axis=1)  26.2 us
    all_to_all x4, local copies, waits for them, and re-layouts, convolve(): lax.all_to_all(stacked.reshape(nfreq_dev, 2, columns), 'freq', split_axis...  24.3 us
    all_gather x1, blocking collectives, local(): lax.all_gather(refl_scale, 'freq', axis=0, tiled=True)  18.6 us
    convert_element_type x2, local copies, waits for them, and re-layouts, local(): to_time(update_cols).astype(jnp.float32)  17.6 us
  transfers between devices with their start and end apart: 4, of which 3 were waited for; matrix products, arithmetic and copies ran while one was open for 10% of the time, Pallas kernels for 0%

commit v1 on v0

--- a/solution.py
+++ b/solution.py
@@ -1,8 +1,20 @@
+import functools
 import math
 import jax
 import jax.numpy as jnp
 from jax import lax
 from jax.sharding import PartitionSpec as P
+
+
+def _measure_hubs(block_in, ndim_at, k_dim):
+    top = jax.lax.axis_size("freq")
+    work_now = jnp.split(block_in, top, ndim_at)
+    piece_next = jnp.stack(work_now, axis=0)
+    carry = jax.lax.all_to_all(piece_next, "freq", 0, 0)
+    return jnp.concatenate(carry, k_dim)
+
+
+define_shelves = functools.partial(_measure_hubs, ndim_at=2, k_dim=0)
 
 
 def to_columns(field):
@@ -66,9 +78,7 @@
         out_r = apply(resp_r, spec_r) - sign * apply(resp_i, spec_i)
         out_i = apply(resp_r, spec_i) + sign * apply(resp_i, spec_r)
         stacked = jnp.stack([out_r.astype(jnp.bfloat16), out_i.astype(jnp.bfloat16)], axis=1)
-        return lax.all_to_all(
-            stacked.reshape(nfreq_dev, 2, columns), "freq", split_axis=2, concat_axis=0, tiled=True
-        )
+        return define_shelves(stacked.reshape(nfreq_dev, 2, columns))
 
     def inverse(spectrum):
         trace = lax.dot_general(

time: 550 us -> 469 us (0.85)
  local copies, waits for them, and re-layouts: 170 us -> 48.4 us
  waiting for transfers between devices: 139 us -> 171 us
  other arithmetic: 13.8 us -> 24.6 us
    unnamed x24 -> x20, local copies, waits for them, and re-layouts: 79.9 us -> 8.75 us
    all_to_all x2, waiting for transfers between devices: 132 us -> 163 us  [to_time(): lax.all_to_all(field, 'freq', split_axis=0, concat_axis=1, tiled=True)]
    another operation x6 -> x4, local copies, waits for them, and re-layouts: 26.2 us -> 0.28 us  [convolve(): jnp.stack([out_r.astype(jnp.bfloat16), out_i.astype(jnp.bfloat16)], axis=1)]
    all_to_all x4 -> x0, local copies, waits for them, and re-layouts: 24.3 us -> none  [convolve(): lax.all_to_all(stacked.reshape(nfreq_dev, 2, columns), 'freq', split_axis...]
    unnamed x0 -> x30, other arithmetic: none -> 10.4 us
  transfers between devices with their start and end apart: 4 -> 4, of which waited for: 3 -> 3; matrix products, arithmetic and copies ran while one was open for 10% -> 5% of each run, Pallas kernels for 0% -> 0%
where the time goes in v1:
time: 469 us; the launch traced here: 462 us
  waiting for transfers between devices  171 us (36%)
  blocking collectives  149 us (32%)
  local copies, waits for them, and re-layouts  48.4 us (10%)
  matrix products  43.1 us (9%)
  starting transfers between devices  24.6 us (5%)
  other arithmetic  24.6 us (5%)
    all_to_all x2, waiting for transfers between devices, to_time(): lax.all_to_all(field, 'freq', split_axis=0, concat_axis=1, tiled=True)  163 us
    unnamed x1, blocking collectives  88.9 us
    all_to_all x2, blocking collectives, forward(): lax.all_to_all(spectrum, 'freq', split_axis=0, concat_axis=2, tiled=True)  28.2 us
    all_gather x1, blocking collectives, local(): lax.all_gather(refl_scale, 'freq', axis=0, tiled=True)  18.6 us
    convert_element_type x2, local copies, waits for them, and re-layouts, local(): to_time(update_cols).astype(jnp.float32)  17.6 us
    dot_general x8, matrix products, apply(): jnp.einsum('frs,fvs->fvr', resp, spec, preferred_element_type=jnp.float32)  15.6 us
    all_to_all x1, blocking collectives, _measure_hubs(): carry = jax.lax.all_to_all(piece_next, 'freq', 0, 0)  12.8 us
    all_to_all x2, starting transfers between devices, to_time(): lax.all_to_all(field, 'freq', split_axis=0, concat_axis=1, tiled=True)  11.7 us
  transfers between devices with their start and end apart: 4, of which 3 were waited for; matrix products, arithmetic and copies ran while one was open for 5% of the time, Pallas kernels for 0%

profile of v1, /device:TPU:11, one launch (start us, length us, event | category | flops | bytes accessed | tf_op | source)
XLA Modules:
  0.0 461.7 jit_solution(12148573190350197899)
XLA Ops:
  0.6 7.9 %copy.35 = bf16[128,32,512]{0,2,1:T(8,128)(2,1)} copy(bf16[128,32,512]{2,1,0:T(8,128)(2,1)} %param.8) | data formatting | bytes 8388608 | tf_op args[3]
  8.5 6.7 %all-to-all-start = ((bf16[128,16,1024]{0,2,1:T(8,128)(2,1)}), bf16[128,16,1024]{0,2,1:T(8,128)(2,1)}, u32[]{:S(2)}, u32[]{:S(2)}) async-start(bf16[128,16,1024]{0,2,1:T(8,128)(2,1)} %bitcast.242), calls=%async_computation | async-start | bytes 8388608 | tf_op jit(solution)/shard_map/all_to_all | solution.py:21
  16.7 88.9 %all-reduce = s32[64]{0:T(128)S(1)} all-reduce(s32[64]{0:T(128)S(1)} %dynamic-update-slice), channel_id=1, replica_groups=mesh['groups'=2,'freq'=16] {'freq'}, use_global_device_ids=true, to_apply=%add | all-reduce | flops 64 | bytes 512
  105.6 18.6 %all-gather = f32[16,4,4]{2,1,0:T(4,128)S(1)} all-gather(f32[1,4,4]{2,1,0:T(4,128)S(1)} %bitcast.254), channel_id=1, replica_groups=mesh['groups'=2,'freq'=16] {'freq'}, dimensions={0}, use_global_device_ids=true | all-gather | bytes 1088 | tf_op jit(solution)/shard_map/all_gather | solution.py:39
  124.5 6.4 %copy.36 = bf16[16,128,1024]{2,1,0:T(8,128)(2,1)} copy(bf16[16,128,1024]{1,2,0:T(8,128)(2,1)} %bitcast.2) | data formatting | bytes 8388608 | tf_op jit(solution)/shard_map/all_to_all | solution.py:21
  130.9 4.5 fusion.64
  135.4 2.5 fusion.65
  138.2 15.2 %all_to_all.88 = bf16[64,2,1024]{2,1,0:T(2,128)(2,1)S(1)} all-to-all(bf16[64,2,1024]{2,1,0:T(2,128)(2,1)S(1)} %copy.37), channel_id=1, replica_groups=mesh['groups'=2,'freq'=16] {'freq'}, dimensions={0} | all-to-all | bytes 524288 | tf_op jit(solution)/shard_map/all_to_all | solution.py:66
  153.7 2.4 fusion.6
  172.0 6.1 %all-to-all-start.2 = ((bf16[16,4,2,1024]{3,2,1,0:T(2,128)(2,1)}), bf16[16,4,2,1024]{3,2,1,0:T(2,128)(2,1)S(1)}, u32[]{:S(2)}, u32[]{:S(2)}) async-start(bf16[16,4,2,1024]{3,2,1,0:T(2,128)(2,1)} %constant_dynamic-update-slice_fusion), calls=%async_computation.2 | async-start | bytes 524288 | tf_op jit(solution)/shard_map/all_to_all | solution.py:13
  178.1 7.9 %all-to-all-done.2 = bf16[16,4,2,1024]{3,2,1,0:T(2,128)(2,1)S(1)} async-done(((bf16[16,4,2,1024]{3,2,1,0:T(2,128)(2,1)}), bf16[16,4,2,1024]{3,2,1,0:T(2,128)(2,1)S(1)}, u32[]{:S(2)}, u32[]{:S(2)}) %all-to-all-start.2) | async-done | bytes 262176 | tf_op jit(solution)/shard_map/all_to_all | solution.py:13
  186.4 3.1 fusion.73
  189.5 4.1 fusion
  193.6 2.5 fusion.62
  196.2 2.5 fusion.63
  199.0 13.0 %all_to_all.89 = bf16[64,2,1024]{2,1,0:T(2,128)(2,1)S(1)} all-to-all(bf16[64,2,1024]{2,1,0:T(2,128)(2,1)S(1)} %copy.44), channel_id=1, replica_groups=mesh['groups'=2,'freq'=16] {'freq'}, dimensions={0} | all-to-all | bytes 524288 | tf_op jit(solution)/shard_map/all_to_all | solution.py:66
  212.3 2.5 fusion.41
  214.8 2.3 fusion.38
  217.9 2.3 fusion.53
  221.2 12.8 %all_to_all.90 = bf16[16,4,2,1024]{3,2,1,0:T(2,128)(2,1)S(1)} all-to-all(bf16[16,4,2,1024]{3,2,1,0:T(2,128)(2,1)S(1)} %constant_dynamic-update-slice_fusion.16), channel_id=1, replica_groups=mesh['groups'=2,'freq'=16] {'freq'}, dimensions={0} | all-to-all | bytes 524288 | tf_op jit(solution)/shard_map/all_to_all | solution.py:13
  234.0 6.5 %all-to-all-start.3 = ((bf16[16,128,1024]{2,1,0:T(8,128)(2,1)}), bf16[16,128,1024]{2,1,0:T(8,128)(2,1)}, u32[]{:S(2)}, u32[]{:S(2)}) async-start(bf16[16,128,1024]{2,1,0:T(8,128)(2,1)} %bitcast.243), calls=%async_computation.3 | async-start | bytes 8388608 | tf_op jit(solution)/shard_map/all_to_all | solution.py:25
  240.8 3.1 fusion.72
  244.0 4.9 %fusion.1 = bf16[2048,1024]{1,0:T(8,128)(2,1)} fusion(f32[2048,1024]{1,0:T(8,128)S(1)} %fusion.72, s32[1024]{0:T(1024)S(1)} %copy-done.5, s32[2048]{0:T(1024)S(1)} %fusion.84, s32[64]{0:T(128)S(1)} %all-reduce, bf16[64,1,1024]{2,1,0:T(2,128)(2,1)S(1)} %get-tuple-element.2), kind=kOutput, calls=%fused_computation.3 | convolution fusion | flops 280887296 | bytes 12726528 | tf_op jit(solution)/shard_map/dot_general | solution.py:87
  248.9 84.1 %all-to-all-done.3 = bf16[16,128,1024]{2,1,0:T(8,128)(2,1)} async-done(((bf16[16,128,1024]{2,1,0:T(8,128)(2,1)}), bf16[16,128,1024]{2,1,0:T(8,128)(2,1)}, u32[]{:S(2)}, u32[]{:S(2)}) %all-to-all-start.3) | async-done | bytes 4194336 | tf_op jit(solution)/shard_map/all_to_all | solution.py:25
  332.9 5.2 %all-to-all-start.6 = ((bf16[16,128,1024]{2,1,0:T(8,128)(2,1)}), bf16[16,128,1024]{2,1,0:T(8,128)(2,1)}, u32[]{:S(2)}, u32[]{:S(2)}) async-start(bf16[16,128,1024]{2,1,0:T(8,128)(2,1)} %bitcast.244), calls=%async_computation.6 | async-start | bytes 8388608 | tf_op jit(solution)/shard_map/all_to_all | solution.py:25
  338.2 6.5 %copy.43 = bf16[128,16,1024]{2,1,0:T(8,128)(2,1)} copy(bf16[128,16,1024]{2,0,1:T(8,128)(2,1)} %bitcast.33) | data formatting | bytes 8388608 | tf_op jit(solution)/shard_map/all_to_all | solution.py:25
  344.7 7.1 %reshape.90 = bf16[128,32,512]{2,1,0:T(8,128)(2,1)} reshape(bf16[128,16,1024]{2,1,0:T(8,128)(2,1)} %copy.43) | data formatting | bytes 8388608 | tf_op jit(solution)/shard_map/reshape | solution.py:97
  351.8 78.7 %all-to-all-done.6 = bf16[16,128,1024]{2,1,0:T(8,128)(2,1)} async-done(((bf16[16,128,1024]{2,1,0:T(8,128)(2,1)}), bf16[16,128,1024]{2,1,0:T(8,128)(2,1)}, u32[]{:S(2)}, u32[]{:S(2)}) %all-to-all-start.6) | async-done | bytes 4194336 | tf_op jit(solution)/shard_map/all_to_all | solution.py:25
  430.5 3.2 convert_bitcast_fusion
  433.7 8.3 %copy.48 = f32[128,16,1024]{2,1,0:T(8,128)} copy(f32[128,16,1024]{2,0,1:T(8,128)S(1)} %convert_bitcast_fusion) | data formatting | bytes 16777216 | tf_op jit(solution)/shard_map/convert_element_type | solution.py:96
  442.0 9.3 %reshape.93 = f32[128,32,512]{2,1,0:T(8,128)} reshape(f32[128,16,1024]{2,1,0:T(8,128)} %copy.48) | data formatting | bytes 16777216 | tf_op jit(solution)/shard_map/convert_element_type | solution.py:96
  451.3 10.2 %convert_add_fusion = f32[128,32,512]{2,1,0:T(8,128)} fusion(f32[128,32,512]{2,1,0:T(8,128)} %reshape.93, bf16[128,32,512]{2,1,0:T(8,128)(2,1)} %param.8), kind=kLoop, calls=%fused_computation.5 | loop fusion | flops 4194304 | bytes 20971520 | tf_op jit(solution)/shard_map/add | solution.py:96
  (73 shorter events, 20.4 us)
Async XLA Ops:
  8.5 6.7 %copy-start.7 = (u32[32]{0:T(128)S(1)}, u32[32]{0:T(128)}, u32[]{:S(2)}) copy-start(u32[32]{0:T(128)} %constant.68) | copy-start | bytes 388
  8.5 8.0 %copy-start.6 = (s32[4]{0:T(128)S(1)}, s32[4]{0:T(128)}, u32[]{:S(2)}) copy-start(s32[4]{0:T(128)} %param.7) | copy-start | bytes 52
  8.5 97.1 %copy-start.4 = (f32[4,4]{1,0:T(4,128)S(1)}, f32[4,4]{1,0:T(4,128)}, u32[]{:S(2)}) copy-start(f32[4,4]{1,0:T(4,128)} %param.6) | copy-start | bytes 196
  8.5 115.9 %all-to-all-start = ((bf16[128,16,1024]{0,2,1:T(8,128)(2,1)}), bf16[128,16,1024]{0,2,1:T(8,128)(2,1)}, u32[]{:S(2)}, u32[]{:S(2)}) async-start(bf16[128,16,1024]{0,2,1:T(8,128)(2,1)} %bitcast.242), calls=%async_computation | async-start | bytes 8388608 | tf_op jit(solution)/shard_map/all_to_all | solution.py:21
  130.9 4.5 copy-start.3
  153.7 4.8 %copy-start = (bf16[4,2,512,512]{3,2,1,0:T(8,128)(2,1)S(1)}, bf16[4,2,512,512]{3,2,1,0:T(8,128)(2,1)}, u32[]{:S(2)}) copy-start(bf16[4,2,512,512]{3,2,1,0:T(8,128)(2,1)} %param.5) | copy-start | bytes 12582916
  172.0 14.0 %all-to-all-start.2 = ((bf16[16,4,2,1024]{3,2,1,0:T(2,128)(2,1)}), bf16[16,4,2,1024]{3,2,1,0:T(2,128)(2,1)S(1)}, u32[]{:S(2)}, u32[]{:S(2)}) async-start(bf16[16,4,2,1024]{3,2,1,0:T(2,128)(2,1)} %constant_dynamic-update-slice_fusion), calls=%async_computation.2 | async-start | bytes 524288 | tf_op jit(solution)/shard_map/all_to_all | solution.py:13
  186.4 3.1 copy-start.5
  193.6 5.1 %copy-start.2 = (bf16[2048,1024]{1,0:T(8,128)(2,1)}, bf16[2048,1024]{1,0:T(8,128)(2,1)S(1)}, u32[]{:S(2)}) copy-start(bf16[2048,1024]{1,0:T(8,128)(2,1)S(1)} %fusion) | copy-start | bytes 12582916
  212.3 4.8 %copy-start.1 = (bf16[4,2,512,512]{3,2,1,0:T(8,128)(2,1)S(1)}, bf16[4,2,512,512]{3,2,1,0:T(8,128)(2,1)}, u32[]{:S(2)}) copy-start(bf16[4,2,512,512]{3,2,1,0:T(8,128)(2,1)} %param.5) | copy-start | bytes 12582916
  234.0 99.0 %all-to-all-start.3 = ((bf16[16,128,1024]{2,1,0:T(8,128)(2,1)}), bf16[16,128,1024]{2,1,0:T(8,128)(2,1)}, u32[]{:S(2)}, u32[]{:S(2)}) async-start(bf16[16,128,1024]{2,1,0:T(8,128)(2,1)} %bitcast.243), calls=%async_computation.3 | async-start | bytes 8388608 | tf_op jit(solution)/shard_map/all_to_all | solution.py:25
  332.9 97.6 %all-to-all-start.6 = ((bf16[16,128,1024]{2,1,0:T(8,128)(2,1)}), bf16[16,128,1024]{2,1,0:T(8,128)(2,1)}, u32[]{:S(2)}, u32[]{:S(2)}) async-start(bf16[16,128,1024]{2,1,0:T(8,128)(2,1)} %bitcast.244), calls=%async_computation.6 | async-start | bytes 8388608 | tf_op jit(solution)/shard_map/all_to_all | solution.py:25
